TPU v7x, 256 devices: a whole 4x4x8 slice. The times are simulated.
256 devices in a mesh: tok: 8 (over z), out: 16 (over y_lo, x, core), grp: 2 (over y_hi).
Axes of the slice: x: 4, y: 4 (y_hi: 2, y_lo: 2; y = y_hi * 2 + y_lo), z: 8, core: 2. Of those that a mesh axis runs over, the one named last changes fastest.
Arguments:
- activations: bfloat16 [2048, 2, 2048], P(('tok', 'grp'), None, 'out'), may hold values from -16 to 16
- out_grads: bfloat16 [2048, 2, 2048], P(('tok', 'grp'), None, 'out'), may hold values from -16 to 16
- weight: bfloat16 [2, 2048, 4096], P(None, 'out'), may hold values from -0.09375 to 0.09375
Outputs:
- update: bfloat16 [4096, 2, 2048], P(('tok', 'grp'), None, 'out')
- input_grad: bfloat16 [2048, 2, 2048], P(('tok', 'grp'), None, 'out')
All inputs are finite; a program needn't handle non-finite values.
Results may differ from a plain program's by a relative error of at most 0.0092.
Values may be sent and summed in bfloat16 or wider, within the bound.
No kernel may reach another device: no remote copies, remote signals or barrier semaphores. Data moves between devices by JAX's collectives and lax.ppermute only.
A program may use at most 64 MiB of HBM per device.

v0:
```python
import math
import jax
import jax.numpy as jnp
from jax import lax
from jax.sharding import Mesh
from jax.sharding import PartitionSpec as P

POWER = 3
OUT = ("out_0", "out_1", "out_2")
TOK_OUT = ("tok", "out_0", "out_1", "out_2")
DAMPING = 0.1
HIGH = lax.Precision.HIGHEST


def own_rows(so_far, axes):
    for axis in axes:
        so_far = lax.psum_scatter(so_far, axis, scatter_dimension=0, tiled=True)
    return so_far


def in_order(pieces, dim):
    lengths = list(pieces.shape[1:])
    lengths[dim] *= pieces.shape[0]
    return jnp.moveaxis(pieces, 0, dim).reshape(lengths)


def copy_for_each(array, axis):
    peers = lax.axis_size(axis)
    return lax.all_to_all(
        jnp.broadcast_to(array[None], (peers, *array.shape)), axis, 0, 0, tiled=True
    )


def gather_directly(array, axis, dim):
    return in_order(copy_for_each(array, axis), dim)


def one_axis_at_a_time(array, axes):
    for axis in axes:
        array = lax.psum(array, axis)
    return array


def swapped(array, axis, stride):
    return lax.ppermute(array, axis, [(i, i ^ 1 << stride) for i in range(lax.axis_size(axis))])


def spread(piece):
    return lax.all_gather(piece, OUT, axis=2, tiled=True)


def token_sums(maker, rows):
    return own_rows(maker(jnp.int32(0), rows * lax.axis_size(("tok", "grp"))), ("tok", "grp"))


def owner_rows(piece):
    return gather_directly(piece, "tok", 0)


def owner_total(vector):
    return one_axis_at_a_time(vector, TOK_OUT)


def diagonal_mask(rows, width, row_start, col_start):
    row_ids = row_start + lax.broadcasted_iota(jnp.int32, (rows, 1, width), 0)
    col_ids = col_start + lax.broadcasted_iota(jnp.int32, (rows, 1, width), 2)
    return jnp.where(row_ids == col_ids, 1.0, 0.0).astype(jnp.float32)


def multiply(left, right, gather_columns):
    row_band = spread(left)
    column_band = gather_columns(right)
    return jnp.einsum("rkj,jkc->rkc", row_band, column_band, preferred_element_type=jnp.float32)


def inverse_roots(tile, row_start, col_start, gather_columns, total):
    rows, count, width = tile.shape
    block = width * lax.axis_size(OUT)
    mask = diagonal_mask(rows, width, row_start, col_start)
    vector = jnp.ones((count, block), jnp.float32)
    image = vector
    for step in range(POWER):
        columns = lax.dynamic_slice_in_dim(vector, col_start, width, 1)
        part = jnp.einsum("rkc,kc->kr", tile, columns, precision=HIGH)
        placed = lax.dynamic_update_slice_in_dim(
            jnp.zeros((count, block), jnp.float32), part, row_start, 1
        )
        image = total(placed)
        if step + 1 < POWER:
            vector = image / jnp.sqrt(jnp.sum(image * image, axis=1, keepdims=True))
    scale = jnp.sum(vector * image, axis=1) / jnp.sum(vector * vector, axis=1)
    start = tile / scale[None, :, None]
    start_low = start.astype(jnp.bfloat16)
    first_low = ((3.0 * mask - start) / 2.0).astype(jnp.bfloat16)
    square_low = multiply(first_low, first_low, gather_columns).astype(jnp.bfloat16)
    moved = multiply(square_low, start_low, gather_columns)
    second_low = ((3.0 * mask - moved) / 2.0).astype(jnp.bfloat16)
    roots = multiply(first_low, second_low, gather_columns) / jnp.sqrt(scale)[None, :, None]
    return roots.astype(jnp.bfloat16)


def local(activations, out_grads, weight):
    tok_dev, blocks, width = activations.shape
    block = width * lax.axis_size(OUT)
    token_count = tok_dev * lax.axis_size("tok") * lax.axis_size("grp")
    col_start = lax.axis_index(OUT) * width
    local_sides = jnp.concatenate([activations, out_grads], axis=1)
    whole_sides = spread(local_sides)
    grads_whole = whole_sides[:, blocks:, :]
    weight_rows = weight.reshape(blocks, width, blocks, block)
    input_grad = jnp.einsum(
        "tjq,bcjq->tbc", grads_whole, weight_rows, preferred_element_type=jnp.float32
    ).astype(jnp.bfloat16)
    rows = block // lax.axis_size("tok")
    row_start = lax.axis_index("tok") * rows
    paired = whole_sides.reshape(tok_dev, 2, blocks, block)
    own_cols = local_sides.reshape(tok_dev, 2, blocks, width)

    def side_terms(start, span):

        def one_group(group):
            side = group % 2
            piece = group // 2
            row_part = lax.dynamic_slice(
                paired, (0, side, 0, piece * rows), (tok_dev, 1, blocks, rows)
            )[:, 0]
            col_part = lax.dynamic_slice(own_cols, (0, side, 0, 0), (tok_dev, 1, blocks, width))[
                :, 0
            ]
            return jnp.einsum(
                "tbr,tbc->rbc", row_part, col_part, preferred_element_type=jnp.float32
            )

        groups = jnp.arange(span // rows, dtype=jnp.int32)
        return lax.map(one_group, groups).reshape(span, blocks, width)

    sums = token_sums(side_terms, rows)
    tile = sums / token_count + DAMPING * diagonal_mask(rows, width, row_start, col_start)
    roots = inverse_roots(tile, row_start, col_start, owner_rows, owner_total)
    own_band = owner_rows(roots)
    other_band = swapped(own_band, "grp", 0)
    first_side = lax.axis_index("grp") == 0
    bands = jnp.concatenate(
        [jnp.where(first_side, own_band, other_band), jnp.where(first_side, other_band, own_band)],
        axis=1,
    )
    whitened = jnp.einsum(
        "tkj,jkc->tkc", whole_sides, bands, preferred_element_type=jnp.float32
    ).astype(jnp.bfloat16)
    acts_whole = spread(whitened[:, :blocks, :]).reshape(tok_dev, blocks * block)
    grads_low = whitened[:, blocks:, :]
    owned_acts = lax.all_to_all(acts_whole, ("tok", "grp"), split_axis=1, concat_axis=0, tiled=True)
    update = jnp.einsum(
        "ta,tbc->abc",
        owned_acts,
        gather_directly(grads_low, ("tok", "grp"), 0),
        preferred_element_type=jnp.float32,
    )
    update = (update / math.sqrt(token_count)).astype(jnp.bfloat16)
    return (update, input_grad)


def solution(mesh):
    split = Mesh(
        mesh.devices.reshape(mesh.shape["tok"], 2, 4, 2, mesh.shape["grp"]),
        ("tok", "out_0", "out_1", "out_2", "grp"),
    )
    in_specs = (P(("tok", "grp"), None, OUT), P(("tok", "grp"), None, OUT), P(None, OUT, None))
    out_specs = (P(("tok", "grp"), None, OUT), P(("tok", "grp"), None, OUT))
    return jax.shard_map(local, mesh=split, in_specs=in_specs, out_specs=out_specs, check_vma=False)
```

profile of v0, /device:TPU:2, one launch (start us, length us, event | category | flops | bytes accessed | tf_op | source)
XLA Modules:
  0.0 650.0 jit_solution(17056723738061298160)
XLA Ops:
  7.2 0.9 copy_dynamic-update-slice_fusion.1
  8.1 0.9 copy_dynamic-update-slice_fusion
  9.7 43.1 %all-gather.5.cloned.1.call-done = bf16[128,4,2048]{2,0,1:T(8,128)(2,1)} async-done(((bf16[128,4,128]{2,0,1:T(8,128)(2,1)}), bf16[128,4,2048]{2,0,1:T(8,128)(2,1)}) %all-gather.5.cloned.1.call-update) | async-done | bytes 2097168 | tf_op jit(solution)/shard_map/all_gather | solution.py:49
  52.8 79.2 %while.12 = (s32[]{:T(128)}, f32[16,256,2,128]{3,1,0,2:T(8,128)}, s32[16]{0:T(128)S(1)}, bf16[128,2,2,128]{3,0,2,1:T(8,128)(2,1)}, bf16[128,2,2,2048]{3,0,2,1:T(...) while((s32[]{:T(128)}, f32[16,256,2,128]{3,1,0,2:T(8,128)}, ...), condition=%wide.region_1.2_spmd, body=%wide.region_0.1_spmd.sunk | while | flops 16777244 | bytes 1509764 | solution.py:135
  55.7 1.2 convolution_bitcast_fusion.4
  60.6 1.2 convolution_bitcast_fusion.4
  61.9 0.7 constant_dynamic-update-slice_fusion.2
  65.6 1.2 convolution_bitcast_fusion.4
  66.9 0.7 constant_dynamic-update-slice_fusion.2
  70.5 1.2 convolution_bitcast_fusion.4
  71.9 0.7 constant_dynamic-update-slice_fusion.2
  75.5 1.2 convolution_bitcast_fusion.4
  80.4 1.2 convolution_bitcast_fusion.4
  81.8 0.7 constant_dynamic-update-slice_fusion.2
  85.4 1.2 convolution_bitcast_fusion.4
  90.3 1.2 convolution_bitcast_fusion.4
  95.3 1.2 convolution_bitcast_fusion.4
  100.2 1.2 convolution_bitcast_fusion.4
  105.2 1.2 convolution_bitcast_fusion.4
  110.1 1.2 convolution_bitcast_fusion.4
  111.4 0.7 constant_dynamic-update-slice_fusion.2
  115.1 1.2 convolution_bitcast_fusion.4
  120.0 1.2 convolution_bitcast_fusion.4
  121.3 0.7 constant_dynamic-update-slice_fusion.2
  125.0 1.2 convolution_bitcast_fusion.4
  129.9 1.2 convolution_bitcast_fusion.4
  131.2 0.8 constant_dynamic-update-slice_fusion.2
  132.1 55.9 %reduce-scatter.3.cloned.1.call-done = f32[512,2,128]{2,0,1:T(8,128)} async-done(((f32[4096,2,128]{2,0,1:T(8,128)}), f32[512,2,128]{2,0,1:T(8,128)}) %reduce-scatter.3.cloned.1.call-update) | async-done | bytes 524304 | tf_op jit(solution)/shard_map/reduce_scatter | solution.py:17
  188.2 22.1 %reduce-scatter.5.cloned.1.call-done = f32[256,2,128]{2,0,1:T(8,128)} async-done(((f32[512,2,128]{2,0,1:T(8,128)}), f32[256,2,128]{2,0,1:T(8,128)}) %reduce-scatter.5.cloned.1.call-update) | async-done | bytes 262160 | tf_op jit(solution)/shard_map/reduce_scatter | solution.py:17
  210.3 1.3 fusion.36
  211.7 30.2 %psum.84 = f32[2,2048]{1,0:T(2,128)S(1)} all-reduce(f32[2,2048]{1,0:T(2,128)S(1)} %bitcast_dynamic-update-slice_fusion.2), channel_id=1, replica_groups=mesh['tok'=8,'out_0'=2,'out_1'=4,'out_2'=2,'grp'=2] {'tok'}, use_global_device_ids=true, to_apply=%region_4.5 | all-reduce | flops 4096 | bytes 32768 | tf_op jit(solution)/shard_map/psum | solution.py:40
  241.9 7.2 %psum.85 = f32[2,2048]{1,0:T(2,128)S(1)} all-reduce(f32[2,2048]{1,0:T(2,128)S(1)} %psum.84), channel_id=1, replica_groups=mesh['tok'=8,'out_0'=2,'out_1'=4,'out_2'=2,'grp'=2] {'out_0'}, use_global_device_ids=true, to_apply=%region_5.6 | all-reduce | flops 4096 | bytes 32768 | tf_op jit(solution)/shard_map/psum | solution.py:40
  249.1 13.9 %psum.86 = f32[2,2048]{1,0:T(2,128)S(1)} all-reduce(f32[2,2048]{1,0:T(2,128)S(1)} %psum.85), channel_id=1, replica_groups=mesh['tok'=8,'out_0'=2,'out_1'=4,'out_2'=2,'grp'=2] {'out_1'}, use_global_device_ids=true, to_apply=%region_6.7 | all-reduce | flops 4096 | bytes 32768 | tf_op jit(solution)/shard_map/psum | solution.py:40
  263.0 3.3 psum.87
  266.6 1.3 fusion.35
  267.9 27.0 %psum.88 = f32[2,2048]{1,0:T(2,128)S(1)} all-reduce(f32[2,2048]{1,0:T(2,128)S(1)} %bitcast_dynamic-update-slice_fusion.1), channel_id=1, replica_groups=mesh['tok'=8,'out_0'=2,'out_1'=4,'out_2'=2,'grp'=2] {'tok'}, use_global_device_ids=true, to_apply=%region_9.10 | all-reduce | flops 4096 | bytes 32768 | tf_op jit(solution)/shard_map/psum | solution.py:40
  295.0 8.1 %psum.89 = f32[2,2048]{1,0:T(2,128)S(1)} all-reduce(f32[2,2048]{1,0:T(2,128)S(1)} %psum.88), channel_id=1, replica_groups=mesh['tok'=8,'out_0'=2,'out_1'=4,'out_2'=2,'grp'=2] {'out_0'}, use_global_device_ids=true, to_apply=%region_10.11 | all-reduce | flops 4096 | bytes 32768 | tf_op jit(solution)/shard_map/psum | solution.py:40
  303.1 16.4 %psum.90 = f32[2,2048]{1,0:T(2,128)S(1)} all-reduce(f32[2,2048]{1,0:T(2,128)S(1)} %psum.89), channel_id=1, replica_groups=mesh['tok'=8,'out_0'=2,'out_1'=4,'out_2'=2,'grp'=2] {'out_1'}, use_global_device_ids=true, to_apply=%region_11.12 | all-reduce | flops 4096 | bytes 32768 | tf_op jit(solution)/shard_map/psum | solution.py:40
  319.5 3.3 psum.91
  323.1 1.3 fusion.34
  324.4 27.6 %psum.92 = f32[2,2048]{1,0:T(2,128)S(1)} all-reduce(f32[2,2048]{1,0:T(2,128)S(1)} %bitcast_dynamic-update-slice_fusion), channel_id=1, replica_groups=mesh['tok'=8,'out_0'=2,'out_1'=4,'out_2'=2,'grp'=2] {'tok'}, use_global_device_ids=true, to_apply=%region_14.15 | all-reduce | flops 4096 | bytes 32768 | tf_op jit(solution)/shard_map/psum | solution.py:40
  352.0 7.2 %psum.93 = f32[2,2048]{1,0:T(2,128)S(1)} all-reduce(f32[2,2048]{1,0:T(2,128)S(1)} %psum.92), channel_id=1, replica_groups=mesh['tok'=8,'out_0'=2,'out_1'=4,'out_2'=2,'grp'=2] {'out_0'}, use_global_device_ids=true, to_apply=%region_15.16 | all-reduce | flops 4096 | bytes 32768 | tf_op jit(solution)/shard_map/psum | solution.py:40
  359.2 14.3 %psum.94 = f32[2,2048]{1,0:T(2,128)S(1)} all-reduce(f32[2,2048]{1,0:T(2,128)S(1)} %psum.93), channel_id=1, replica_groups=mesh['tok'=8,'out_0'=2,'out_1'=4,'out_2'=2,'grp'=2] {'out_1'}, use_global_device_ids=true, to_apply=%region_16.17 | all-reduce | flops 4096 | bytes 32768 | tf_op jit(solution)/shard_map/psum | solution.py:40
  373.5 3.3 psum.95
  377.0 1.7 multiply_convert_fusion
  378.8 1.0 copy.52
  380.0 33.4 %all_to_all.41 = bf16[8,256,2,128]{1,3,2,0:T(8,128)(2,1)S(1)} all-to-all(bf16[8,256,2,128]{1,3,2,0:T(8,128)(2,1)S(1)} %broadcast_in_dim.58), channel_id=1, replica_groups=mesh['tok'=8,'out_0'=2,'out_1'=4,'out_2'=2,'grp'=2] {'tok'}, dimensions={0} | all-to-all | bytes 2097152 | tf_op jit(solution)/shard_map/all_to_all | solution.py:29
  413.5 2.6 all-gather.7.cloned.1.call-done
  416.1 3.1 fusion.21
  419.5 35.9 %all_to_all.42 = bf16[8,256,2,128]{1,3,2,0:T(8,128)(2,1)S(1)} all-to-all(bf16[8,256,2,128]{1,3,2,0:T(8,128)(2,1)S(1)} %broadcast_in_dim.57), channel_id=1, replica_groups=mesh['tok'=8,'out_0'=2,'out_1'=4,'out_2'=2,'grp'=2] {'tok'}, dimensions={0} | all-to-all | bytes 2097152 | tf_op jit(solution)/shard_map/all_to_all | solution.py:29
  455.7 2.6 fusion.17
  458.5 36.1 %all_to_all.43 = bf16[8,256,2,128]{1,3,2,0:T(8,128)(2,1)S(1)} all-to-all(bf16[8,256,2,128]{1,3,2,0:T(8,128)(2,1)S(1)} %broadcast_in_dim.59), channel_id=1, replica_groups=mesh['tok'=8,'out_0'=2,'out_1'=4,'out_2'=2,'grp'=2] {'tok'}, dimensions={0} | all-to-all | bytes 2097152 | tf_op jit(solution)/shard_map/all_to_all | solution.py:29
  494.7 0.8 fusion.28
  495.7 31.0 %all_to_all.44 = bf16[8,256,2,128]{1,3,2,0:T(8,128)(2,1)S(1)} all-to-all(bf16[8,256,2,128]{1,3,2,0:T(8,128)(2,1)S(1)} %broadcast_in_dim.60), channel_id=1, replica_groups=mesh['tok'=8,'out_0'=2,'out_1'=4,'out_2'=2,'grp'=2] {'tok'}, dimensions={0} | all-to-all | bytes 2097152 | tf_op jit(solution)/shard_map/all_to_all | solution.py:29
  526.8 2.9 collective-permute-start
  529.7 21.7 %collective-permute-done = bf16[2048,2,128]{0,2,1:T(8,128)(2,1)S(1)} collective-permute-done((bf16[2048,2,128]{0,2,1:T(8,128)(2,1)S(1)}, bf16[2048,2,128]{0,2,1:T(8,128)(2,1)S(1)}, u32[]{:S(2)}, u32[]{:S(2)}) %collective-permute-start) | collective-permute-done | bytes 1048608 | tf_op jit(solution)/shard_map/ppermute | solution.py:45
  553.0 1.3 broadcast_in_dim.61
  554.2 5.5 all-to-all-start.5
  560.3 27.3 %all-to-all-done.5 = bf16[16,128,2,128]{3,1,2,0:T(8,128)(2,1)S(1)} async-done(((bf16[16,128,2,128]{3,1,2,0:T(8,128)(2,1)}), bf16[16,128,2,128]{3,1,2,0:T(8,128)(2,1)S(1)}, u32[]{:S(2)}, u32[]{:S(2)}) %all-to-all-start.5) | async-done | bytes 1048608 | tf_op jit(solution)/shard_map/all_to_all | solution.py:29
  587.6 13.5 %all-gather.11.cloned.1.call-done = bf16[128,2,2048]{0,2,1:T(8,128)(2,1)} async-done(((bf16[128,2,128]{0,2,1:T(8,128)(2,1)}), bf16[128,2,2048]{0,2,1:T(8,128)(2,1)}) %all-gather.11.cloned.1.call-update) | async-done | bytes 1048592 | tf_op jit(solution)/shard_map/all_gather | solution.py:49
  601.0 10.3 %all-to-all-start.4 = ((bf16[128,16,256]{0,2,1:T(8,128)(2,1)}), bf16[128,16,256]{0,2,1:T(8,128)(2,1)S(1)}, u32[]{:S(2)}, u32[]{:S(2)}) async-start(bf16[128,16,256]{0,2,1:T(8,128)(2,1)} %bitcast.112), calls=%async_computation.6 | async-start | bytes 2097152 | tf_op jit(solution)/shard_map/all_to_all | solution.py:152
  611.3 2.8 fusion.29
  614.8 27.2 %all-to-all-done.4 = bf16[128,16,256]{0,2,1:T(8,128)(2,1)S(1)} async-done(((bf16[128,16,256]{0,2,1:T(8,128)(2,1)}), bf16[128,16,256]{0,2,1:T(8,128)(2,1)S(1)}, u32[]{:S(2)}, u32[]{:S(2)}) %all-to-all-start.4) | async-done | bytes 1048608 | tf_op jit(solution)/shard_map/all_to_all | solution.py:152
  642.4 0.8 copy.62
  (97 shorter events, 24.2 us)
Async XLA Ops:
  7.2 45.6 %all-gather.5.cloned.1.call-start = ((), (), s32[]{:S(2)}) async-start(), calls=%async_computation.8 | async-start | bytes 2228224 | tf_op jit(solution)/shard_map/all_gather | solution.py:49
  8.9 0.7 copy-start.1
  9.6 178.4 %reduce-scatter.3.cloned.1.call-start = ((), (), s32[]{:S(2)}) async-start(), calls=%async_computation.9 | async-start | bytes 4718592 | tf_op jit(solution)/shard_map/reduce_scatter | solution.py:17
  132.0 78.3 %reduce-scatter.5.cloned.1.call-start = ((), (), s32[]{:S(2)}) async-start(), calls=%async_computation.10 | async-start | bytes 786432 | tf_op jit(solution)/shard_map/reduce_scatter | solution.py:17
  188.0 228.1 %all-gather.7.cloned.1.call-start = ((), (), s32[]{:S(2)}) async-start(), calls=%async_computation.11 | async-start | bytes 2228224 | tf_op jit(solution)/shard_map/all_gather | solution.py:49
  378.8 76.9 %all-gather.9.cloned.1.call-start = ((), (), s32[]{:S(2)}) async-start(), calls=%async_computation.12 | async-start | bytes 2228224 | tf_op jit(solution)/shard_map/all_gather | solution.py:49
  458.5 36.2 %copy-start = (bf16[256,2,2048]{2,0,1:T(8,128)(2,1)S(1)}, bf16[256,2,2048]{2,0,1:T(8,128)(2,1)}, u32[]{:S(2)}) copy-start(bf16[256,2,2048]{2,0,1:T(8,128)(2,1)} %all-gather.7.cloned.1.call-done) | copy-start | bytes 6291460
  526.8 24.5 %collective-permute-start = (bf16[2048,2,128]{0,2,1:T(8,128)(2,1)S(1)}, bf16[2048,2,128]{0,2,1:T(8,128)(2,1)S(1)}, u32[]{:S(2)}, u32[]{:S(2)}) collective-permute-start(bf16[2048,2,128]{0,2,1:T(8,128)(2,1)S(1)} %bitcast.102), channel_id=1, source_target_pairs={{0,1},{1,0},{2,3},{3,2},{4,5},{5,4},{6,7},{7,6},{8,9},{9,8},{10,11... | collective-permute-start | bytes 3145736 | tf_op jit(solution)/shard_map/ppermute | solution.py:45
  529.7 21.8 %copy-start.2 = (bf16[128,2,2,2048]{3,0,2,1:T(8,128)(2,1)S(1)}, bf16[128,2,2,2048]{3,0,2,1:T(8,128)(2,1)}, u32[]{:S(2)}) copy-start(bf16[128,2,2,2048]{3,0,2,1:T(8,128)(2,1)} %get-tuple-element.215) | copy-start | bytes 6291460
  554.2 33.3 %all-to-all-start.5 = ((bf16[16,128,2,128]{3,1,2,0:T(8,128)(2,1)}), bf16[16,128,2,128]{3,1,2,0:T(8,128)(2,1)S(1)}, u32[]{:S(2)}, u32[]{:S(2)}) async-start(bf16[16,128,2,128]{3,1,2,0:T(8,128)(2,1)} %broadcast_in_dim.61), calls=%async_computation.7 | async-start | bytes 2097152 | tf_op jit(solution)/shard_map/all_to_all | solution.py:29
  559.7 41.3 %all-gather.11.cloned.1.call-start = ((), (), s32[]{:S(2)}) async-start(), calls=%async_computation.13 | async-start | bytes 1114112 | tf_op jit(solution)/shard_map/all_gather | solution.py:49
  601.0 40.9 %all-to-all-start.4 = ((bf16[128,16,256]{0,2,1:T(8,128)(2,1)}), bf16[128,16,256]{0,2,1:T(8,128)(2,1)S(1)}, u32[]{:S(2)}, u32[]{:S(2)}) async-start(bf16[128,16,256]{0,2,1:T(8,128)(2,1)} %bitcast.112), calls=%async_computation.6 | async-start | bytes 2097152 | tf_op jit(solution)/shard_map/all_to_all | solution.py:152
Sparse Core Ops, SparseCore 0:
  10.3 42.3 all-gather.4
  132.1 55.8 reduce-scatter.2
  190.5 19.7 reduce-scatter.4
  378.9 37.1 all-gather.6
  419.4 36.2 all-gather.8
  562.8 38.2 all-gather.10
where the time goes:
time: 652 us; the launch traced here: 650 us
  blocking collectives  298 us (46%)
  waiting for transfers between devices  214 us (33%)
  loops' own time  37.5 us (6%)
  matrix products  33 us (5%)
  local copies, waits for them, and re-layouts  31.1 us (5%)
  starting transfers between devices  18.8 us (3%)
  between operations  14.4 us (2%)
    psum x12, blocking collectives, one_axis_at_a_time(): array = lax.psum(array, axis)  162 us
    all_to_all x4, blocking collectives, copy_for_each(): lax.all_to_all(jnp.broadcast_to(array[None], (peers, *array.shape)), axis...  136 us
    reduce_scatter x2, waiting for transfers between devices, own_rows(): so_far = lax.psum_scatter(so_far, axis, scatter_dimension=0, tiled=True)  78.1 us
    all_gather x4, waiting for transfers between devices, spread(): return lax.all_gather(piece, OUT, axis=2, tiled=True)  59.4 us
    another operation x1, loops' own time, side_terms(): return lax.map(one_group, groups).reshape(span, blocks, width)  37.5 us
    all_to_all x1, waiting for transfers between devices, copy_for_each(): lax.all_to_all(jnp.broadcast_to(array[None], (peers, *array.shape)), axis...  27.3 us
    all_to_all x1, waiting for transfers between devices, local(): lax.all_to_all(acts_whole, ('tok', 'grp'), split_axis=1, concat_axis=0, t...  27.2 us
    ppermute x1, waiting for transfers between devices, swapped(): lax.ppermute(array, axis, [(i, i ^ 1 << stride) for i in range(lax.axis_s...  21.7 us
  transfers between devices with their start and end apart: 9, of which 9 were waited for; matrix products, arithmetic and copies ran while one was open for 1% of the time, Pallas kernels for 0%

commit v1 on v0

--- a/solution.py
+++ b/solution.py
@@ -37,7 +37,12 @@
 
 def one_axis_at_a_time(array, axes):
     for axis in axes:
-        array = lax.psum(array, axis)
+
+        def state_circles(peer_axis, mine_x):
+            main = lax.all_gather(mine_x, axis_name=peer_axis).sum(axis=0)
+            return main
+
+        array = state_circles(axis, array)
     return array
 
 

time: 652 us -> 618 us (0.948)
  blocking collectives: 298 us -> 267 us
    psum x12 -> x0, blocking collectives: 162 us -> none  [one_axis_at_a_time(): array = lax.psum(array, axis)]
    all_gather x0 -> x12, blocking collectives: none -> 130 us  [state_circles(): main = lax.all_gather(mine_x, axis_name=peer_axis).sum(axis=0)]
where the time goes in v1:
time: 618 us; the launch traced here: 616 us
  blocking collectives  267 us (43%)
  waiting for transfers between devices  213 us (34%)
  loops' own time  37.5 us (6%)
  matrix products  32.1 us (5%)
  local copies, waits for them, and re-layouts  31.1 us (5%)
  starting transfers between devices  18.8 us (3%)
  between operations  14.4 us (2%)
    all_to_all x4, blocking collectives, copy_for_each(): lax.all_to_all(jnp.broadcast_to(array[None], (peers, *array.shape)), axis...  138 us
    all_gather x12, blocking collectives, state_circles(): main = lax.all_gather(mine_x, axis_name=peer_axis).sum(axis=0)  130 us
    reduce_scatter x2, waiting for transfers between devices, own_rows(): so_far = lax.psum_scatter(so_far, axis, scatter_dimension=0, tiled=True)  78.1 us
    all_gather x4, waiting for transfers between devices, spread(): return lax.all_gather(piece, OUT, axis=2, tiled=True)  58.6 us
    another operation x1, loops' own time, side_terms(): return lax.map(one_group, groups).reshape(span, blocks, width)  37.5 us
    all_to_all x1, waiting for transfers between devices, copy_for_each(): lax.all_to_all(jnp.broadcast_to(array[None], (peers, *array.shape)), axis...  27.3 us
    all_to_all x1, waiting for transfers between devices, local(): lax.all_to_all(acts_whole, ('tok', 'grp'), split_axis=1, concat_axis=0, t...  27.2 us
    ppermute x1, waiting for transfers between devices, swapped(): lax.ppermute(array, axis, [(i, i ^ 1 << stride) for i in range(lax.axis_s...  21.6 us
  transfers between devices with their start and end apart: 9, of which 9 were waited for; matrix products, arithmetic and copies ran while one was open for 1% of the time, Pallas kernels for 0%

profile of v1, /device:TPU:2, one launch (start us, length us, event | category | flops | bytes accessed | tf_op | source)
XLA Modules:
  0.0 616.4 jit_solution(6681882134788316795)
XLA Ops:
  7.2 0.9 copy_dynamic-update-slice_fusion.1
  8.1 0.9 copy_dynamic-update-slice_fusion
  9.7 43.1 %all-gather.23.cloned.1.call-done = bf16[128,4,2048]{2,0,1:T(8,128)(2,1)} async-done(((bf16[128,4,128]{2,0,1:T(8,128)(2,1)}), bf16[128,4,2048]{2,0,1:T(8,128)(2,1)}) %all-gather.23.cloned.1.call-update) | async-done | bytes 2097168 | tf_op jit(solution)/shard_map/all_gather | solution.py:54
  52.8 79.2 %while.12 = (s32[]{:T(128)}, f32[16,256,2,128]{3,1,0,2:T(8,128)}, s32[16]{0:T(128)S(1)}, bf16[128,2,2,128]{3,0,2,1:T(8,128)(2,1)}, bf16[128,2,2,2048]{3,0,2,1:T(...) while((s32[]{:T(128)}, f32[16,256,2,128]{3,1,0,2:T(8,128)}, ...), condition=%wide.region_1.2_spmd, body=%wide.region_0.1_spmd.sunk | while | flops 16777244 | bytes 1509764 | solution.py:140
  55.7 1.2 convolution_bitcast_fusion.4
  60.6 1.2 convolution_bitcast_fusion.4
  61.9 0.7 constant_dynamic-update-slice_fusion.2
  65.6 1.2 convolution_bitcast_fusion.4
  66.9 0.7 constant_dynamic-update-slice_fusion.2
  70.5 1.2 convolution_bitcast_fusion.4
  71.9 0.7 constant_dynamic-update-slice_fusion.2
  75.5 1.2 convolution_bitcast_fusion.4
  80.4 1.2 convolution_bitcast_fusion.4
  81.8 0.7 constant_dynamic-update-slice_fusion.2
  85.4 1.2 convolution_bitcast_fusion.4
  90.3 1.2 convolution_bitcast_fusion.4
  95.3 1.2 convolution_bitcast_fusion.4
  96.6 0.7 constant_dynamic-update-slice_fusion.2
  100.2 1.2 convolution_bitcast_fusion.4
  105.2 1.2 convolution_bitcast_fusion.4
  110.1 1.2 convolution_bitcast_fusion.4
  111.4 0.7 constant_dynamic-update-slice_fusion.2
  115.1 1.2 convolution_bitcast_fusion.4
  120.0 1.2 convolution_bitcast_fusion.4
  121.3 0.7 constant_dynamic-update-slice_fusion.2
  125.0 1.2 convolution_bitcast_fusion.4
  129.9 1.2 convolution_bitcast_fusion.4
  131.2 0.8 constant_dynamic-update-slice_fusion.2
  132.1 55.9 %reduce-scatter.3.cloned.1.call-done = f32[512,2,128]{2,0,1:T(8,128)} async-done(((f32[4096,2,128]{2,0,1:T(8,128)}), f32[512,2,128]{2,0,1:T(8,128)}) %reduce-scatter.3.cloned.1.call-update) | async-done | bytes 524304 | tf_op jit(solution)/shard_map/reduce_scatter | solution.py:17
  188.2 22.1 %reduce-scatter.5.cloned.1.call-done = f32[256,2,128]{2,0,1:T(8,128)} async-done(((f32[512,2,128]{2,0,1:T(8,128)}), f32[256,2,128]{2,0,1:T(8,128)}) %reduce-scatter.5.cloned.1.call-update) | async-done | bytes 262160 | tf_op jit(solution)/shard_map/reduce_scatter | solution.py:17
  210.3 1.4 fusion.36
  211.8 26.0 %all_gather.90 = f32[8,2,2048]{2,1,0:T(2,128)S(1)} all-gather(f32[1,2,2048]{2,1,0:T(2,128)S(1)} %bitcast_dynamic-update-slice_fusion.2), channel_id=1, replica_groups=mesh['tok'=8,'out_0'=2,'out_1'=4,'out_2'=2,'grp'=2] {'tok'}, dimensions={0}, use_global_device_ids=true | all-gather | bytes 147456 | tf_op jit(solution)/shard_map/all_gather | solution.py:42
  237.8 4.4 all-gather.9
  242.3 11.9 %all-gather.10 = f32[4,2,2048]{2,1,0:T(2,128)S(1)} all-gather(f32[1,2,2048]{2,1,0:T(2,128)S(1)} %bitcast.130), channel_id=3, replica_groups=mesh['tok'=8,'out_0'=2,'out_1'=4,'out_2'=2,'grp'=2] {'out_1'}, dimensions={0}, use_global_device_ids=true | all-gather | bytes 81920 | tf_op jit(solution)/shard_map/all_gather | solution.py:42
  254.2 1.8 all-gather.11
  256.2 1.3 fusion.35
  257.6 24.6 %all_gather.98 = f32[8,2,2048]{2,1,0:T(2,128)S(1)} all-gather(f32[1,2,2048]{2,1,0:T(2,128)S(1)} %bitcast_dynamic-update-slice_fusion.1), channel_id=1, replica_groups=mesh['tok'=8,'out_0'=2,'out_1'=4,'out_2'=2,'grp'=2] {'tok'}, dimensions={0}, use_global_device_ids=true | all-gather | bytes 147456 | tf_op jit(solution)/shard_map/all_gather | solution.py:42
  282.2 4.4 all-gather.12
  286.7 11.9 %all-gather.13 = f32[4,2,2048]{2,1,0:T(2,128)S(1)} all-gather(f32[1,2,2048]{2,1,0:T(2,128)S(1)} %bitcast.133), channel_id=6, replica_groups=mesh['tok'=8,'out_0'=2,'out_1'=4,'out_2'=2,'grp'=2] {'out_1'}, dimensions={0}, use_global_device_ids=true | all-gather | bytes 81920 | tf_op jit(solution)/shard_map/all_gather | solution.py:42
  298.5 1.8 all-gather.14
  301.0 24.6 %all_gather.106 = f32[8,2,2048]{2,1,0:T(2,128)S(1)} all-gather(f32[1,2,2048]{2,1,0:T(2,128)S(1)} %bitcast_dynamic-update-slice_fusion), channel_id=1, replica_groups=mesh['tok'=8,'out_0'=2,'out_1'=4,'out_2'=2,'grp'=2] {'tok'}, dimensions={0}, use_global_device_ids=true | all-gather | bytes 147456 | tf_op jit(solution)/shard_map/all_gather | solution.py:42
  325.7 4.4 all-gather.15
  330.1 11.9 %all-gather.16 = f32[4,2,2048]{2,1,0:T(2,128)S(1)} all-gather(f32[1,2,2048]{2,1,0:T(2,128)S(1)} %bitcast.136), channel_id=9, replica_groups=mesh['tok'=8,'out_0'=2,'out_1'=4,'out_2'=2,'grp'=2] {'out_1'}, dimensions={0}, use_global_device_ids=true | all-gather | bytes 81920 | tf_op jit(solution)/shard_map/all_gather | solution.py:42
  342.0 1.8 all-gather.17
  344.1 0.8 multiply_convert_fusion
  344.9 1.0 copy.52
  346.0 34.5 %all_to_all.41 = bf16[8,256,2,128]{1,3,2,0:T(8,128)(2,1)S(1)} all-to-all(bf16[8,256,2,128]{1,3,2,0:T(8,128)(2,1)S(1)} %broadcast_in_dim.58), channel_id=1, replica_groups=mesh['tok'=8,'out_0'=2,'out_1'=4,'out_2'=2,'grp'=2] {'tok'}, dimensions={0} | all-to-all | bytes 2097152 | tf_op jit(solution)/shard_map/all_to_all | solution.py:29
  380.7 1.8 all-gather.25.cloned.1.call-done
  382.4 3.1 fusion.21
  385.8 35.9 %all_to_all.42 = bf16[8,256,2,128]{1,3,2,0:T(8,128)(2,1)S(1)} all-to-all(bf16[8,256,2,128]{1,3,2,0:T(8,128)(2,1)S(1)} %broadcast_in_dim.57), channel_id=1, replica_groups=mesh['tok'=8,'out_0'=2,'out_1'=4,'out_2'=2,'grp'=2] {'tok'}, dimensions={0} | all-to-all | bytes 2097152 | tf_op jit(solution)/shard_map/all_to_all | solution.py:29
  422.1 2.6 fusion.17
  424.9 36.1 %all_to_all.43 = bf16[8,256,2,128]{1,3,2,0:T(8,128)(2,1)S(1)} all-to-all(bf16[8,256,2,128]{1,3,2,0:T(8,128)(2,1)S(1)} %broadcast_in_dim.59), channel_id=1, replica_groups=mesh['tok'=8,'out_0'=2,'out_1'=4,'out_2'=2,'grp'=2] {'tok'}, dimensions={0} | all-to-all | bytes 2097152 | tf_op jit(solution)/shard_map/all_to_all | solution.py:29
  461.1 0.8 fusion.28
  462.0 31.0 %all_to_all.44 = bf16[8,256,2,128]{1,3,2,0:T(8,128)(2,1)S(1)} all-to-all(bf16[8,256,2,128]{1,3,2,0:T(8,128)(2,1)S(1)} %broadcast_in_dim.60), channel_id=1, replica_groups=mesh['tok'=8,'out_0'=2,'out_1'=4,'out_2'=2,'grp'=2] {'tok'}, dimensions={0} | all-to-all | bytes 2097152 | tf_op jit(solution)/shard_map/all_to_all | solution.py:29
  493.2 2.9 collective-permute-start
  496.0 21.6 %collective-permute-done = bf16[2048,2,128]{0,2,1:T(8,128)(2,1)S(1)} collective-permute-done((bf16[2048,2,128]{0,2,1:T(8,128)(2,1)S(1)}, bf16[2048,2,128]{0,2,1:T(8,128)(2,1)S(1)}, u32[]{:S(2)}, u32[]{:S(2)}) %collective-permute-start) | collective-permute-done | bytes 1048608 | tf_op jit(solution)/shard_map/ppermute | solution.py:50
  519.3 1.3 broadcast_in_dim.61
  520.6 5.5 all-to-all-start.5
  526.7 27.3 %all-to-all-done.5 = bf16[16,128,2,128]{3,1,2,0:T(8,128)(2,1)S(1)} async-done(((bf16[16,128,2,128]{3,1,2,0:T(8,128)(2,1)}), bf16[16,128,2,128]{3,1,2,0:T(8,128)(2,1)S(1)}, u32[]{:S(2)}, u32[]{:S(2)}) %all-to-all-start.5) | async-done | bytes 1048608 | tf_op jit(solution)/shard_map/all_to_all | solution.py:29
  553.9 13.5 %all-gather.29.cloned.1.call-done = bf16[128,2,2048]{0,2,1:T(8,128)(2,1)} async-done(((bf16[128,2,128]{0,2,1:T(8,128)(2,1)}), bf16[128,2,2048]{0,2,1:T(8,128)(2,1)}) %all-gather.29.cloned.1.call-update) | async-done | bytes 1048592 | tf_op jit(solution)/shard_map/all_gather | solution.py:54
  567.4 10.3 %all-to-all-start.4 = ((bf16[128,16,256]{0,2,1:T(8,128)(2,1)}), bf16[128,16,256]{0,2,1:T(8,128)(2,1)S(1)}, u32[]{:S(2)}, u32[]{:S(2)}) async-start(bf16[128,16,256]{0,2,1:T(8,128)(2,1)} %bitcast.124), calls=%async_computation.6 | async-start | bytes 2097152 | tf_op jit(solution)/shard_map/all_to_all | solution.py:157
  577.7 2.8 fusion.29
  581.2 27.2 %all-to-all-done.4 = bf16[128,16,256]{0,2,1:T(8,128)(2,1)S(1)} async-done(((bf16[128,16,256]{0,2,1:T(8,128)(2,1)}), bf16[128,16,256]{0,2,1:T(8,128)(2,1)S(1)}, u32[]{:S(2)}, u32[]{:S(2)}) %all-to-all-start.4) | async-done | bytes 1048608 | tf_op jit(solution)/shard_map/all_to_all | solution.py:157
  608.8 0.8 copy.62
  (111 shorter events, 24.2 us)
Async XLA Ops:
  7.2 45.6 %all-gather.23.cloned.1.call-start = ((), (), s32[]{:S(2)}) async-start(), calls=%async_computation.8 | async-start | bytes 2228224 | tf_op jit(solution)/shard_map/all_gather | solution.py:54
  8.9 0.7 copy-start.2
  9.6 178.4 %reduce-scatter.3.cloned.1.call-start = ((), (), s32[]{:S(2)}) async-start(), calls=%async_computation.9 | async-start | bytes 4718592 | tf_op jit(solution)/shard_map/reduce_scatter | solution.py:17
  132.0 78.3 %reduce-scatter.5.cloned.1.call-start = ((), (), s32[]{:S(2)}) async-start(), calls=%async_computation.10 | async-start | bytes 786432 | tf_op jit(solution)/shard_map/reduce_scatter | solution.py:17
  188.0 194.4 %all-gather.25.cloned.1.call-start = ((), (), s32[]{:S(2)}) async-start(), calls=%async_computation.11 | async-start | bytes 2228224 | tf_op jit(solution)/shard_map/all_gather | solution.py:54
  210.3 90.3 %copy-start = (f32[256,2,128]{2,0,1:T(8,128)S(1)}, f32[256,2,128]{2,0,1:T(8,128)}, u32[]{:S(2)}) copy-start(f32[256,2,128]{2,0,1:T(8,128)} %reduce-scatter.5.cloned.1.call-done) | copy-start | bytes 786436
  344.9 77.2 %all-gather.27.cloned.1.call-start = ((), (), s32[]{:S(2)}) async-start(), calls=%async_computation.12 | async-start | bytes 2228224 | tf_op jit(solution)/shard_map/all_gather | solution.py:54
  424.9 36.2 %copy-start.1 = (bf16[256,2,2048]{2,0,1:T(8,128)(2,1)S(1)}, bf16[256,2,2048]{2,0,1:T(8,128)(2,1)}, u32[]{:S(2)}) copy-start(bf16[256,2,2048]{2,0,1:T(8,128)(2,1)} %all-gather.25.cloned.1.call-done) | copy-start | bytes 6291460
  493.2 24.5 %collective-permute-start = (bf16[2048,2,128]{0,2,1:T(8,128)(2,1)S(1)}, bf16[2048,2,128]{0,2,1:T(8,128)(2,1)S(1)}, u32[]{:S(2)}, u32[]{:S(2)}) collective-permute-start(bf16[2048,2,128]{0,2,1:T(8,128)(2,1)S(1)} %bitcast.114), channel_id=1, source_target_pairs={{0,1},{1,0},{2,3},{3,2},{4,5},{5,4},{6,7},{7,6},{8,9},{9,8},{10,11... | collective-permute-start | bytes 3145736 | tf_op jit(solution)/shard_map/ppermute | solution.py:50
  496.0 21.8 %copy-start.3 = (bf16[128,2,2,2048]{3,0,2,1:T(8,128)(2,1)S(1)}, bf16[128,2,2,2048]{3,0,2,1:T(8,128)(2,1)}, u32[]{:S(2)}) copy-start(bf16[128,2,2,2048]{3,0,2,1:T(8,128)(2,1)} %get-tuple-element.215) | copy-start | bytes 6291460
  520.6 33.3 %all-to-all-start.5 = ((bf16[16,128,2,128]{3,1,2,0:T(8,128)(2,1)}), bf16[16,128,2,128]{3,1,2,0:T(8,128)(2,1)S(1)}, u32[]{:S(2)}, u32[]{:S(2)}) async-start(bf16[16,128,2,128]{3,1,2,0:T(8,128)(2,1)} %broadcast_in_dim.61), calls=%async_computation.7 | async-start | bytes 2097152 | tf_op jit(solution)/shard_map/all_to_all | solution.py:29
  526.1 41.3 %all-gather.29.cloned.1.call-start = ((), (), s32[]{:S(2)}) async-start(), calls=%async_computation.13 | async-start | bytes 1114112 | tf_op jit(solution)/shard_map/all_gather | solution.py:54
  567.4 40.9 %all-to-all-start.4 = ((bf16[128,16,256]{0,2,1:T(8,128)(2,1)}), bf16[128,16,256]{0,2,1:T(8,128)(2,1)S(1)}, u32[]{:S(2)}, u32[]{:S(2)}) async-start(bf16[128,16,256]{0,2,1:T(8,128)(2,1)} %bitcast.124), calls=%async_computation.6 | async-start | bytes 2097152 | tf_op jit(solution)/shard_map/all_to_all | solution.py:157
Sparse Core Ops, SparseCore 0:
  10.3 42.3 all-gather.22
  132.1 55.8 reduce-scatter.2
  190.5 19.7 reduce-scatter.4
  345.0 37.3 all-gather.24
  385.7 36.3 all-gather.26
  529.1 38.2 all-gather.28
